TPU v7x, 32 devices: a whole 2x2x4 slice. The times are simulated.
32 devices in a mesh: dp: 8 (over z, core), tensor: 4 (over y, x).
Axes of the slice: x: 2, y: 2, z: 4, core: 2. Of those that a mesh axis runs over, the one named last changes fastest.
Arguments:
- out_grad: bfloat16 [8192, 1024], P('dp'), may hold values from -6 to 6
- hidden: bfloat16 [8192, 8192], P('dp', 'tensor'), may hold values from -6 to 6
- error_buffer: bfloat16 [8192, 8192], P('dp', 'tensor'), may hold values from -6 to 6
- right_factor: float32 [8192, 64], P('tensor'), may hold values from -6 to 6
Outputs:
- error_next: bfloat16 [8192, 8192], P('dp', 'tensor')
- factor_next: float32 [8192, 64], P('tensor')
All inputs are finite; a program needn't handle non-finite values.
Results may differ from a plain program's by a relative error of at most 0.001.
Values sent between devices are 32-bit elements; how exact they have to be, the bound alone decides.
No kernel may reach another device: no remote copies, remote signals or barrier semaphores. Data moves between devices by JAX's collectives and lax.ppermute only.
A program may use at most 64 MiB of HBM per device.

v0:
```python
import jax
import jax.numpy as jnp
from jax import lax
from jax.sharding import PartitionSpec as P


def right_terms(columns, basis):
    return lax.dot_general(
        columns, basis, (((0,), (0,)), ((), ())), precision=lax.Precision.HIGHEST
    )


def body(out_grad, hidden, error_buffer, right_factor):
    tok_rows = hidden.shape[0]
    gradient = lax.dot_general(
        out_grad, hidden, (((0,), (0,)), ((), ())), preferred_element_type=jnp.float32
    )
    merged = gradient * tok_rows ** (-0.5) + error_buffer.astype(jnp.float32)
    local_left = jnp.dot(merged, right_factor, precision=lax.Precision.HIGHEST)
    row_share = lax.psum_scatter(local_left, "tensor", scatter_dimension=0, tiled=True)
    row_share = lax.psum(row_share, "dp")
    gram_local = jnp.dot(row_share.T, row_share, precision=lax.Precision.HIGHEST)
    gram_matrix = lax.psum(gram_local, "tensor")
    factor_lower = jnp.linalg.cholesky(gram_matrix)
    solved = jax.scipy.linalg.solve_triangular(factor_lower, row_share.T, lower=True).T
    basis = lax.all_gather(solved, "tensor", axis=0, tiled=True)
    replicas = lax.axis_size("dp")
    factor_next = lax.psum(right_terms(merged, basis), "dp") / replicas
    approx = jnp.dot(basis, factor_next.T, precision=lax.Precision.HIGHEST)
    error_next = (merged - approx).astype(jnp.bfloat16)
    return (error_next, factor_next)


def solution(mesh):
    placed = (P("dp", None), P("dp", "tensor"), P("dp", "tensor"), P("tensor", None))
    return jax.shard_map(
        body,
        mesh=mesh,
        in_specs=placed,
        out_specs=(P("dp", "tensor"), P("tensor", None)),
        check_vma=False,
    )
```

profile of v0, /device:TPU:0, one launch (start us, length us, event | category | flops | bytes accessed | tf_op | source)
XLA Modules:
  0.0 234.0 jit_solution(9764179374427362821)
XLA Ops:
  7.2 0.0 reduce-scatter.2.cloned.1.call-start
  7.2 1.5 copy-done
  8.8 8.0 %convert_add_fusion = f32[1024,2048]{1,0:T(8,128)S(1)} fusion(bf16[1024,2048]{1,0:T(8,128)(2,1)} %param.6, bf16[1024,1024]{1,0:T(8,128)(2,1)S(1)} %copy-done, bf16[1024,2048]{1,0:T(8,128)(2,1)} %param.5), kind=kOutput, calls=%fused_computation.1 | convolution fusion | flops 4301258752 | bytes 18874368 | tf_op jit(solution)/shard_map/dot_general | solution.py:15
  16.8 3.2 %copy-done.1 = f32[1024,2048]{1,0:T(8,128)} copy-done((f32[1024,2048]{1,0:T(8,128)}, f32[1024,2048]{1,0:T(8,128)S(1)}, u32[]{:S(2)}) %copy-start.1) | copy-done | bytes 8388632
  20.0 9.0 %fusion.4 = f32[1024,64]{0,1:T(8,128)} fusion(f32[1024,2048]{1,0:T(8,128)S(1)} %convert_add_fusion, f32[2048,64]{0,1:T(8,128)S(1)} %copy-done.3), kind=kOutput, calls=%fused_computation.13 | convolution fusion | flops 1610612736 | bytes 9175040 | tf_op jit(solution)/shard_map/dot_general | solution.py:19
  29.0 0.0 reduce-scatter.2.cloned.1.call-update
  29.0 0.0 all-reduce.3.cloned.1.call-start
  29.0 27.1 %reduce-scatter.2.cloned.1.call-done = f32[256,64]{0,1:T(8,128)} async-done(((f32[1024,64]{0,1:T(8,128)}), f32[256,64]{0,1:T(8,128)}) %reduce-scatter.2.cloned.1.call-update) | async-done | bytes 65552 | tf_op jit(solution)/shard_map/reduce_scatter | solution.py:20
  56.2 0.0 all-reduce.5.cloned.1.call-start
  56.3 57.0 %all-reduce.3.cloned.1.call-done = f32[256,64]{0,1:T(8,128)} async-done(((f32[256,64]{0,1:T(8,128)}), f32[256,64]{0,1:T(8,128)}) %all-reduce.3.cloned.1.call-update) | async-done | bytes 65552 | tf_op jit(solution)/shard_map/psum | solution.py:21
  113.2 1.1 fusion.5
  114.3 16.2 %psum.22 = f32[64,64]{0,1:T(8,128)S(1)} all-reduce(f32[64,64]{0,1:T(8,128)S(1)} %fusion.5), channel_id=1, replica_groups=mesh['dp'=8,'tensor'=4] {'tensor'}, use_global_device_ids=true, to_apply=%region_2.0 | all-reduce | flops 4096 | bytes 32768 | tf_op jit(solution)/shard_map/psum | solution.py:23
  130.6 0.1 copy.7
  130.7 5.8 %cholesky.16 = f32[64,64]{1,0:T(8,128)S(1)} custom-call(f32[64,64]{1,0:T(8,128)S(1)} %fusion.3), custom_call_target="Cholesky" | custom-call | tf_op jit(solution)/shard_map/jit(cholesky)/cholesky | solution.py:24
  136.5 0.6 compare_reduce_fusion
  137.2 0.7 fusion
  137.9 4.9 %custom-call.7 = f32[1,64,64]{1,2,0:T(8,128)S(1)} custom-call(f32[1,64,64]{2,1,0:T(8,128)S(1)} %fusion), custom_call_target="InvertDiagBlocksLowerTriangular" | custom-call | tf_op jit(solution)/shard_map/jit(_solve_triangular)/triangular_solve | solution.py:25
  142.7 1.1 fusion.1
  143.9 8.2 %all_gather.3 = f32[1024,64]{0,1:T(8,128)S(1)} all-gather(f32[256,64]{0,1:T(8,128)S(1)} %fusion.1), channel_id=1, replica_groups=mesh['dp'=8,'tensor'=4] {'tensor'}, dimensions={0}, use_global_device_ids=true | all-gather | bytes 327680 | tf_op jit(solution)/shard_map/all_gather | solution.py:26
  152.1 8.6 %fusion.6 = f32[2048,64]{0,1:T(8,128)} fusion(f32[1024,2048]{1,0:T(8,128)} %copy-done.1, f32[1024,64]{0,1:T(8,128)S(1)} %all_gather.3), kind=kOutput, calls=%fused_computation.15 | convolution fusion | flops 1610612736 | bytes 9175040 | tf_op jit(solution)/shard_map/dot_general | solution.py:8
  160.7 0.0 all-reduce.5.cloned.1.call-update
  160.8 54.8 %all-reduce.5.cloned.1.call-done = f32[2048,64]{0,1:T(8,128)} async-done(((f32[2048,64]{0,1:T(8,128)}), f32[2048,64]{0,1:T(8,128)}) %all-reduce.5.cloned.1.call-update) | async-done | bytes 524304 | tf_op jit(solution)/shard_map/psum | solution.py:28
  215.6 1.1 broadcast_multiply_fusion
  216.7 10.8 %subtract_convert_fusion = bf16[1024,2048]{1,0:T(8,128)(2,1)} fusion(f32[1024,2048]{1,0:T(8,128)} %copy-done.1, f32[1024,64]{0,1:T(8,128)S(1)} %all_gather.3, f32[2048,64]{0,1:T(8,128)S(1)} %broadcast_multiply_fusion), kind=kOutput, calls=%fused_computation | convolution fusion | flops 1614807040 | bytes 13369344 | tf_op jit(solution)/shard_map/dot_general | solution.py:29
  (9 shorter events, 0.1 us)
Async XLA Ops:
  7.2 1.6 copy-start
  7.2 12.8 %copy-start.3 = (f32[2048,64]{0,1:T(8,128)S(1)}, f32[2048,64]{0,1:T(8,128)}, u32[]{:S(2)}) copy-start(f32[2048,64]{0,1:T(8,128)} %param.7) | copy-start | bytes 1572868
  7.2 49.0 %reduce-scatter.2.cloned.1.call-start = ((), (), s32[]{:S(2)}) async-start(), calls=%async_computation.1 | async-start | bytes 327680 | tf_op jit(solution)/shard_map/reduce_scatter | solution.py:20
  16.8 3.2 %copy-start.1 = (f32[1024,2048]{1,0:T(8,128)}, f32[1024,2048]{1,0:T(8,128)S(1)}, u32[]{:S(2)}) copy-start(f32[1024,2048]{1,0:T(8,128)S(1)} %convert_add_fusion) | copy-start | bytes 25165828
  29.0 84.2 %all-reduce.3.cloned.1.call-start = ((), (), s32[]{:S(2)}) async-start(), calls=%async_computation.2 | async-start | bytes 131072 | tf_op jit(solution)/shard_map/psum | solution.py:21
  56.2 159.4 %all-reduce.5.cloned.1.call-start = ((), (), s32[]{:S(2)}) async-start(), calls=%async_computation.3 | async-start | bytes 1048576 | tf_op jit(solution)/shard_map/psum | solution.py:28
  216.7 10.8 %copy-start.2 = (f32[2048,64]{0,1:T(8,128)}, f32[2048,64]{0,1:T(8,128)S(1)}, u32[]{:S(2)}) copy-start(f32[2048,64]{0,1:T(8,128)S(1)} %broadcast_multiply_fusion) | copy-start | bytes 1572868
Sparse Core Ops, SparseCore 0:
  29.1 27.0 reduce-scatter.1
  58.5 54.6 all-reduce.2
  160.9 54.6 all-reduce.4
where the time goes:
time: 234 us
  waiting for transfers between devices  139 us (59%)
  matrix products  38.6 us (16%)
  blocking collectives  24.5 us (10%)
  between operations  13.8 us (6%)
  other arithmetic  13.2 us (6%)
  local copies, waits for them, and re-layouts  4.83 us (2%)
    psum x1, waiting for transfers between devices, body(): row_share = lax.psum(row_share, 'dp')  57 us
    psum x1, waiting for transfers between devices, body(): factor_next = lax.psum(right_terms(merged, basis), 'dp') / replicas  54.8 us
    reduce_scatter x1, waiting for transfers between devices, body(): lax.psum_scatter(local_left, 'tensor', scatter_dimension=0, tiled=True)  27.1 us
    psum x1, blocking collectives, body(): gram_matrix = lax.psum(gram_local, 'tensor')  16.2 us
    dot_general x1, matrix products, body(): approx = jnp.dot(basis, factor_next.T, precision=lax.Precision.HIGHEST)  10.8 us
    dot_general x1, matrix products, body(): local_left = jnp.dot(merged, right_factor, precision=lax.Precision.HIGHEST)  8.96 us
    dot_general x1, matrix products, right_terms(): lax.dot_general(columns, basis, (((0,), (0,)), ((), ())), precision=lax.P...  8.63 us
    all_gather x1, blocking collectives, body(): basis = lax.all_gather(solved, 'tensor', axis=0, tiled=True)  8.25 us
  transfers between devices with their start and end apart: 3, of which 3 were waited for; matrix products, arithmetic and copies ran while one was open for 0% of the time, Pallas kernels for 0%

commit v1 on v0

v1 whole, which is shorter than its diff:
```python
import functools

import jax
import jax.numpy as jnp
from jax import lax
from jax.experimental import pallas as pl
from jax.experimental.pallas import tpu as pltpu
from jax.sharding import PartitionSpec as P

F32 = jnp.float32
BF16 = jnp.bfloat16
AXES = ("dp", "tensor")
HIGHEST = lax.Precision.HIGHEST


def halves(value):
    high = value.astype(BF16)
    return high, (value - high.astype(F32)).astype(BF16)


def dot(left, right, dims=(1, 0), precision=None):
    return lax.dot_general(
        left,
        right,
        (((dims[0],), (dims[1],)), ((), ())),
        precision=precision,
        preferred_element_type=F32,
    )


def low_lanes(shape, rank):
    return lax.broadcasted_iota(jnp.int32, shape, 1) < rank


def merge_kernel(scale, rank, rows_at_once, grad_ref, hid_ref, err_ref, rt_ref,
                 high_ref, low_ref, left_ref, gt_ref, acc_ref):
    step = pl.program_id(0)
    rows = gt_ref.shape[0]

    @pl.when(step == 0)
    def _():
        for at in range(0, rows, rows_at_once):
            gt_ref[at : at + rows_at_once, :] = grad_ref[:, at : at + rows_at_once].T
        acc_ref[...] = jnp.zeros_like(acc_ref)

    r_high, r_low = halves(rt_ref[...])
    r_both = jnp.concatenate([r_high, r_low], axis=0)
    for at in range(0, rows, rows_at_once):
        here = slice(at, at + rows_at_once)
        gradient = dot(gt_ref[here, :], hid_ref[...])
        merged = gradient * scale + err_ref[here, :].astype(F32)
        high, low = halves(merged)
        high_ref[here, :] = high
        low_ref[here, :] = low
        acc_ref[here, :] += dot(high, r_both, (1, 1)) + dot(low, r_both, (1, 1))

    @pl.when(step == pl.num_programs(0) - 1)
    def _():
        left = acc_ref[...]
        left = left + pltpu.roll(left, rank, 1)
        half = rows // 2
        first = low_lanes((half, 2 * rank), rank)
        left_ref[...] = jnp.where(first, left[:half], left[half:])


def merge(out_grad, hidden, error_buffer, right_t, tile):
    tok, rows = out_grad.shape
    columns = hidden.shape[1]
    rank = right_t.shape[0]
    return pl.pallas_call(
        functools.partial(merge_kernel, tok ** (-0.5), rank, min(256, rows)),
        grid=(columns // tile,),
        in_specs=[
            pl.BlockSpec((tok, rows), lambda j: (0, 0), pipeline_mode=pl.Buffered(1)),
            pl.BlockSpec((tok, tile), lambda j: (0, j)),
            pl.BlockSpec((rows, tile), lambda j: (0, j)),
            pl.BlockSpec((rank, tile), lambda j: (0, j)),
        ],
        out_specs=[
            pl.BlockSpec((rows, tile), lambda j: (0, j)),
            pl.BlockSpec((rows, tile), lambda j: (0, j)),
            pl.BlockSpec((rows // 2, 2 * rank), lambda j: (0, 0)),
        ],
        out_shape=[
            jax.ShapeDtypeStruct((rows, columns), BF16),
            jax.ShapeDtypeStruct((rows, columns), BF16),
            jax.ShapeDtypeStruct((rows // 2, 2 * rank), F32),
        ],
        scratch_shapes=[pltpu.VMEM((rows, tok), BF16), pltpu.VMEM((rows, 2 * rank), F32)],
        compiler_params=pltpu.CompilerParams(vmem_limit_bytes=32 << 20),
        name="merge",
    )(out_grad, hidden, error_buffer, right_t)


def right_kernel(rank, left_ref, high_ref, low_ref, out_ref, lt_ref):
    @pl.when(pl.program_id(0) == 0)
    def _():
        both = left_ref[...].T
        left_t = jnp.concatenate([both[:rank], both[rank:]], axis=1)
        high, low = halves(left_t)
        lt_ref[:rank, :] = high
        lt_ref[rank:, :] = low

    terms = dot(lt_ref[...], high_ref[...]) + dot(lt_ref[...], low_ref[...])
    out_ref[...] = terms[:rank] + terms[rank:]


def right_terms(left, high, low, rank, tile):
    rows, columns = high.shape
    return pl.pallas_call(
        functools.partial(right_kernel, rank),
        grid=(columns // tile,),
        in_specs=[
            pl.BlockSpec(left.shape, lambda j: (0, 0), pipeline_mode=pl.Buffered(1)),
            pl.BlockSpec((rows, tile), lambda j: (0, j)),
            pl.BlockSpec((rows, tile), lambda j: (0, j)),
        ],
        out_specs=pl.BlockSpec((rank, tile), lambda j: (0, j)),
        out_shape=jax.ShapeDtypeStruct((rank, columns), F32),
        scratch_shapes=[pltpu.VMEM((2 * rank, rows), BF16)],
        compiler_params=pltpu.CompilerParams(vmem_limit_bytes=16 << 20),
        name="right_terms",
    )(left, high, low)


def factor_kernel(rank, left_ref, out_ref):
    left = left_ref[...]
    gram = dot(left, left, (0, 0), HIGHEST)
    gram = gram[:rank, :rank] + gram[rank:, rank:]
    row = lax.broadcasted_iota(jnp.int32, (rank, 1), 0)
    eye = (
        lax.broadcasted_iota(jnp.int32, (rank, rank), 0)
        == lax.broadcasted_iota(jnp.int32, (rank, rank), 1)
    ).astype(F32)
    work = jnp.concatenate([gram, eye], axis=1)
    for k in range(rank):
        scale = lax.rsqrt(work[k : k + 1, k : k + 1])
        pivot = work[k : k + 1, :] * scale
        column = work[:, k : k + 1] * scale
        work = jnp.where(row > k, work - column * pivot, work)
        work = jnp.where(row == k, pivot, work)
    out_ref[...] = work[:, rank:]


def factor(left, rank):
    return pl.pallas_call(
        functools.partial(factor_kernel, rank),
        out_shape=jax.ShapeDtypeStruct((rank, rank), F32),
        compiler_params=pltpu.CompilerParams(vmem_limit_bytes=8 << 20),
        name="factor",
    )(left)


def finish_kernel(rank, replicas, rows_at_once, left_ref, inverse_ref, sum_ref, high_ref,
                  low_ref, error_ref, next_ref, lp_ref):
    rows = high_ref.shape[0]

    @pl.when(pl.program_id(0) == 0)
    def _():
        half = rows // 2
        left = left_ref[...]
        first = low_lanes(left.shape, rank)
        other = pltpu.roll(left, rank, 1)
        for at, mine in ((0, left), (half, other)):
            high, low = halves(mine)
            moved = pltpu.roll(low.astype(F32), rank, 1)
            lp_ref[at : at + half, : 2 * rank] = jnp.where(first, high.astype(F32), moved).astype(BF16)
            lp_ref[at : at + half, 2 * rank :] = jnp.where(first, high.astype(F32), 0.0).astype(BF16)

    inverse = inverse_ref[...]
    factor_next = dot(inverse, sum_ref[...], (1, 0), HIGHEST) * (1.0 / replicas)
    next_ref[...] = factor_next
    weight = dot(inverse, factor_next, (0, 0), HIGHEST)
    high, low = halves(weight)
    weights = jnp.concatenate([high, high, low, jnp.zeros_like(low)], axis=0)
    for at in range(0, rows, rows_at_once):
        here = slice(at, at + rows_at_once)
        approx = dot(lp_ref[here, :], weights)
        merged = high_ref[here, :].astype(F32) + low_ref[here, :].astype(F32)
        error_ref[here, :] = (merged - approx).astype(BF16)


def finish(left, inverse, right_sum, high, low, replicas, tile):
    rows, columns = high.shape
    rank = inverse.shape[0]
    return pl.pallas_call(
        functools.partial(finish_kernel, rank, replicas, min(256, rows)),
        grid=(columns // tile,),
        in_specs=[
            pl.BlockSpec(left.shape, lambda j: (0, 0), pipeline_mode=pl.Buffered(1)),
            pl.BlockSpec(inverse.shape, lambda j: (0, 0), pipeline_mode=pl.Buffered(1)),
            pl.BlockSpec((rank, tile), lambda j: (0, j)),
            pl.BlockSpec((rows, tile), lambda j: (0, j)),
            pl.BlockSpec((rows, tile), lambda j: (0, j)),
        ],
        out_specs=[
            pl.BlockSpec((rows, tile), lambda j: (0, j)),
            pl.BlockSpec((rank, tile), lambda j: (0, j)),
        ],
        out_shape=[
            jax.ShapeDtypeStruct((rows, columns), BF16),
            jax.ShapeDtypeStruct((rank, columns), F32),
        ],
        scratch_shapes=[pltpu.VMEM((rows, 4 * rank), BF16)],
        compiler_params=pltpu.CompilerParams(vmem_limit_bytes=24 << 20),
        name="finish",
    )(left, inverse, right_sum, high, low)


def exchange(value, mask, devices):
    return lax.ppermute(value, AXES, [(i, i ^ mask) for i in range(devices)])


def scatter_half(value, mask, devices, upper):
    half = value.shape[0] // 2
    keep = jnp.where(upper, value[half:], value[:half])
    give = jnp.where(upper, value[:half], value[half:])
    return keep + exchange(give, mask, devices)


def gather_half(value, mask, devices, upper):
    other = exchange(value, mask, devices)
    return jnp.concatenate(
        [jnp.where(upper, other, value), jnp.where(upper, value, other)], axis=0
    )


def bits(start, stop):
    masks = []
    while start < stop:
        masks.append(start)
        start *= 2
    return masks


def all_sum(value, scattered, exchanged, devices):
    where = lax.axis_index(AXES)
    upper = [(where & mask) != 0 for mask in scattered]
    for mask, up in zip(scattered, upper):
        value = scatter_half(value, mask, devices, up)
    for mask in exchanged:
        value = value + exchange(value, mask, devices)
    for mask, up in reversed(list(zip(scattered, upper))):
        value = gather_half(value, mask, devices, up)
    return value


def body(out_grad, hidden, error_buffer, right_factor):
    replicas, shards = lax.axis_size("dp"), lax.axis_size("tensor")
    devices = replicas * shards
    rank = right_factor.shape[1]
    tile = 256
    high, low, left = merge(out_grad, hidden, error_buffer, right_factor.T, tile)
    tensor_bits, dp_bits = bits(1, shards), bits(shards, devices)
    left = all_sum(left, [dp_bits[0], tensor_bits[0]], tensor_bits[1:] + dp_bits[1:], devices)
    right_sum = right_terms(left, high, low, rank, tile)
    inverse = factor(left, rank)
    right_sum = all_sum(right_sum, dp_bits[:2], dp_bits[2:], devices)
    error_next, factor_next = finish(left, inverse, right_sum, high, low, replicas, tile)
    return (error_next, factor_next.T)


def solution(mesh):
    placed = (P("dp", None), P("dp", "tensor"), P("dp", "tensor"), P("tensor", None))
    return jax.shard_map(
        body,
        mesh=mesh,
        in_specs=placed,
        out_specs=(P("dp", "tensor"), P("tensor", None)),
        check_vma=False,
    )
```

time: 234 us -> 105 us (0.45)
  waiting for transfers between devices: 139 us -> 30.1 us
  matrix products: 38.6 us -> 0 us
  Pallas kernels: 0 us -> 37.4 us
  blocking collectives: 24.5 us -> 0 us
  starting transfers between devices: 0.12 us -> 18.2 us
  between operations: 13.8 us -> 0.84 us
  other arithmetic: 13.2 us -> 0.39 us
  local copies, waits for them, and re-layouts: 4.83 us -> 17.5 us
    psum x2 -> x0, waiting for transfers between devices: 112 us -> none  [the longest x1 57 us: body(): row_share = lax.psum(row_share, 'dp')]
    dot_general x5 -> x0, matrix products: 37.5 us -> none  [the longest x1 10.8 us: body(): approx = jnp.dot(basis, factor_next.T, precision=lax.Precision.HIGHEST)]
    pallas_call x0 -> x4, Pallas kernels: none -> 37.4 us  [the longest x1 19.4 us: merge(): pl.pallas_call(functools.partial(merge_kernel, tok ** (-0.5), rank, min(2...]
    ppermute x0 -> x12, waiting for transfers between devices: none -> 30.1 us  [exchange(): return lax.ppermute(value, AXES, [(i, i ^ mask) for i in range(devices)])]
    reduce_scatter x1 -> x0, waiting for transfers between devices: 27.1 us -> none  [body(): lax.psum_scatter(local_left, 'tensor', scatter_dimension=0, tiled=True)]
    ppermute x0 -> x12, starting transfers between devices: none -> 18.2 us  [exchange(): return lax.ppermute(value, AXES, [(i, i ^ mask) for i in range(devices)])]
    psum x1 -> x0, blocking collectives: 16.2 us -> none  [body(): gram_matrix = lax.psum(gram_local, 'tensor')]
    unnamed x8 -> x20, local copies, waits for them, and re-layouts: 4.76 us -> 17.5 us
  transfers between devices with their start and end apart: 3 -> 12, of which waited for: 3 -> 11; matrix products, arithmetic and copies ran while one was open for 0% -> 0% of each run, Pallas kernels for 0% -> 6%
where the time goes in v1:
time: 105 us
  Pallas kernels  37.4 us (36%)
  waiting for transfers between devices  30.1 us (29%)
  starting transfers between devices  18.2 us (17%)
  local copies, waits for them, and re-layouts  17.5 us (17%)
    ppermute x12, waiting for transfers between devices, exchange(): return lax.ppermute(value, AXES, [(i, i ^ mask) for i in range(devices)])  30.1 us
    pallas_call x1, Pallas kernels, merge(): pl.pallas_call(functools.partial(merge_kernel, tok ** (-0.5), rank, min(2...  19.4 us
    ppermute x12, starting transfers between devices, exchange(): return lax.ppermute(value, AXES, [(i, i ^ mask) for i in range(devices)])  18.2 us
    unnamed x20, local copies, waits for them, and re-layouts  17.5 us
    pallas_call x1, Pallas kernels, finish(): pl.pallas_call(functools.partial(finish_kernel, rank, replicas, min(256,...  8.21 us
    pallas_call x1, Pallas kernels, factor(): pl.pallas_call(functools.partial(factor_kernel, rank), out_shape=jax.Shap...  5.88 us
    pallas_call x1, Pallas kernels, right_terms(): pl.pallas_call(functools.partial(right_kernel, rank), grid=(columns // ti...  3.97 us
  transfers between devices with their start and end apart: 12, of which 11 were waited for; matrix products, arithmetic and copies ran while one was open for 0% of the time, Pallas kernels for 6%

profile of v1, /device:TPU:0, one launch (start us, length us, event | category | flops | bytes accessed | tf_op | source)
XLA Modules:
  0.0 104.5 jit_solution(16428916377874856780)
XLA Ops:
  0.6 2.2 %copy-done.6 = bf16[1024,2048]{1,0:T(8,128)(2,1)S(1)} copy-done((bf16[1024,2048]{1,0:T(8,128)(2,1)S(1)}, bf16[1024,2048]{1,0:T(8,128)(2,1)}, u32[]{:S(2)}) %copy-start.6) | copy-done | bytes 4194328
  2.8 2.2 %copy-done.7 = bf16[1024,2048]{1,0:T(8,128)(2,1)S(1)} copy-done((bf16[1024,2048]{1,0:T(8,128)(2,1)S(1)}, bf16[1024,2048]{1,0:T(8,128)(2,1)}, u32[]{:S(2)}) %copy-start.7) | copy-done | bytes 4194328
  7.7 19.4 %merge.1 = (bf16[1024,2048]{1,0:T(8,128)(2,1)S(1)}, bf16[1024,2048]{1,0:T(8,128)(2,1)S(1)}, f32[512,128]{1,0:T(8,128)S(1)}) custom-call(bf16[1024,1024]{1,0:T(8,128)(2,1)S(1)} %copy-done.8, bf16[1024,2048]{1,0:T(8,128)(2,1)S(1)} %copy-done.6, bf16[1024,2048]{1,0:T(8,128)(2,1)S(1)} %copy-done.7, f32[64,2048]{1,0:T(8,128)S(1)} %bitcast.2), custom_call_target="tpu_custom_call" | custom-call | tf_op jit(solution)/shard_map/merge/pallas_call | solution.py:70
  27.0 2.0 %copy-done = bf16[1024,2048]{1,0:T(8,128)(2,1)} copy-done((bf16[1024,2048]{1,0:T(8,128)(2,1)}, bf16[1024,2048]{1,0:T(8,128)(2,1)S(1)}, u32[]{:S(2)}) %copy-start) | copy-done | bytes 4194328
  29.0 1.9 %copy-done.3 = bf16[1024,2048]{1,0:T(8,128)(2,1)} copy-done((bf16[1024,2048]{1,0:T(8,128)(2,1)}, bf16[1024,2048]{1,0:T(8,128)(2,1)S(1)}, u32[]{:S(2)}) %copy-start.3) | copy-done | bytes 4194328
  32.6 2.9 %collective-permute-start.1 = (f32[128,128]{1,0:T(8,128)S(1)}, f32[128,128]{1,0:T(8,128)S(1)}, u32[]{:S(2)}, u32[]{:S(2)}) collective-permute-start(f32[128,128]{1,0:T(8,128)S(1)} %slice_select_fusion.3), channel_id=1, source_target_pairs={{0,1},{1,0},{2,3},{3,2},{4,5},{5,4},{6,7},{7,6},{8,9},{9,8},{10,11... | collective-permute-start | bytes 196616 | tf_op jit(solution)/shard_map/ppermute | solution.py:211
  35.5 2.4 %collective-permute-done.1 = f32[128,128]{1,0:T(8,128)S(1)} collective-permute-done((f32[128,128]{1,0:T(8,128)S(1)}, f32[128,128]{1,0:T(8,128)S(1)}, u32[]{:S(2)}, u32[]{:S(2)}) %collective-permute-start.1) | collective-permute-done | bytes 65568 | tf_op jit(solution)/shard_map/ppermute | solution.py:211
  37.9 2.0 %collective-permute-start.2 = (f32[128,128]{1,0:T(8,128)S(1)}, f32[128,128]{1,0:T(8,128)S(1)}, u32[]{:S(2)}, u32[]{:S(2)}) collective-permute-start(f32[128,128]{1,0:T(8,128)S(1)} %select_add_fusion.3), channel_id=1, source_target_pairs={{0,2},{1,3},{2,0},{3,1},{4,6},{5,7},{6,4},{7,5},{8,10},{9,11},{10,... | collective-permute-start | bytes 196616 | tf_op jit(solution)/shard_map/ppermute | solution.py:211
  39.9 2.4 %collective-permute-done.2 = f32[128,128]{1,0:T(8,128)S(1)} collective-permute-done((f32[128,128]{1,0:T(8,128)S(1)}, f32[128,128]{1,0:T(8,128)S(1)}, u32[]{:S(2)}, u32[]{:S(2)}) %collective-permute-start.2) | collective-permute-done | bytes 65568 | tf_op jit(solution)/shard_map/ppermute | solution.py:211
  42.3 2.0 %collective-permute-start.3 = (f32[128,128]{1,0:T(8,128)S(1)}, f32[128,128]{1,0:T(8,128)S(1)}, u32[]{:S(2)}, u32[]{:S(2)}) collective-permute-start(f32[128,128]{1,0:T(8,128)S(1)} %add.31), channel_id=1, source_target_pairs={{0,8},{1,9},{2,10},{3,11},{4,12},{5,13},{6,14},{7,15},{8,0},{9,1},... | collective-permute-start | bytes 196616 | tf_op jit(solution)/shard_map/ppermute | solution.py:211
  44.3 2.3 %collective-permute-done.3 = f32[128,128]{1,0:T(8,128)S(1)} collective-permute-done((f32[128,128]{1,0:T(8,128)S(1)}, f32[128,128]{1,0:T(8,128)S(1)}, u32[]{:S(2)}, u32[]{:S(2)}) %collective-permute-start.3) | collective-permute-done | bytes 65568 | tf_op jit(solution)/shard_map/ppermute | solution.py:211
  46.6 3.7 %collective-permute-start.4 = (f32[128,128]{1,0:T(8,128)S(1)}, f32[128,128]{1,0:T(8,128)S(1)}, u32[]{:S(2)}, u32[]{:S(2)}) collective-permute-start(f32[128,128]{1,0:T(8,128)S(1)} %add.32), channel_id=1, source_target_pairs={{0,16},{1,17},{2,18},{3,19},{4,20},{5,21},{6,22},{7,23},{8,24},{9,... | collective-permute-start | bytes 196616 | tf_op jit(solution)/shard_map/ppermute | solution.py:211
  50.3 2.3 %collective-permute-done.4 = f32[128,128]{1,0:T(8,128)S(1)} collective-permute-done((f32[128,128]{1,0:T(8,128)S(1)}, f32[128,128]{1,0:T(8,128)S(1)}, u32[]{:S(2)}, u32[]{:S(2)}) %collective-permute-start.4) | collective-permute-done | bytes 65568 | tf_op jit(solution)/shard_map/ppermute | solution.py:211
  54.1 2.8 %collective-permute-done.5 = f32[128,128]{1,0:T(8,128)S(1)} collective-permute-done((f32[128,128]{1,0:T(8,128)S(1)}, f32[128,128]{1,0:T(8,128)S(1)}, u32[]{:S(2)}, u32[]{:S(2)}) %collective-permute-start.5) | collective-permute-done | bytes 65568 | tf_op jit(solution)/shard_map/ppermute | solution.py:211
  58.4 2.2 %copy-done.1 = bf16[1024,2048]{1,0:T(8,128)(2,1)S(1)} copy-done((bf16[1024,2048]{1,0:T(8,128)(2,1)S(1)}, bf16[1024,2048]{1,0:T(8,128)(2,1)}, u32[]{:S(2)}) %copy-start.1) | copy-done | bytes 4194328
  60.6 2.2 %copy-done.4 = bf16[1024,2048]{1,0:T(8,128)(2,1)S(1)} copy-done((bf16[1024,2048]{1,0:T(8,128)(2,1)S(1)}, bf16[1024,2048]{1,0:T(8,128)(2,1)}, u32[]{:S(2)}) %copy-start.4) | copy-done | bytes 4194328
  62.8 4.0 %right_terms.1 = f32[64,2048]{1,0:T(8,128)S(1)} custom-call(f32[512,128]{1,0:T(8,128)S(1)} %pad_maximum_fusion.1.left_ref, bf16[1024,2048]{1,0:T(8,128)(2,1)S(1)} %copy-done.1, bf16[1024,2048]{1,0:T(8,128)(2,1)S(1)} %copy-done.4), custom_call_target="tpu_custom_call" | custom-call | tf_op jit(solution)/shard_map/right_terms/pallas_call | solution.py:110
  69.8 4.3 %collective-permute-done.8 = f32[16,2048]{1,0:T(8,128)S(1)} collective-permute-done((f32[16,2048]{1,0:T(8,128)S(1)}, f32[16,2048]{1,0:T(8,128)S(1)}, u32[]{:S(2)}, u32[]{:S(2)}) %collective-permute-start.8) | collective-permute-done | bytes 131104 | tf_op jit(solution)/shard_map/ppermute | solution.py:211
  74.1 3.1 %collective-permute-start.9 = (f32[16,2048]{1,0:T(8,128)S(1)}, f32[16,2048]{1,0:T(8,128)S(1)}, u32[]{:S(2)}, u32[]{:S(2)}) collective-permute-start(f32[16,2048]{1,0:T(8,128)S(1)} %select_add_fusion.1), channel_id=1, source_target_pairs={{0,16},{1,17},{2,18},{3,19},{4,20},{5,21},{6,22},{7,23},{8,24},{9,... | collective-permute-start | bytes 393224 | tf_op jit(solution)/shard_map/ppermute | solution.py:211
  77.2 5.8 %collective-permute-done.9 = f32[16,2048]{1,0:T(8,128)S(1)} collective-permute-done((f32[16,2048]{1,0:T(8,128)S(1)}, f32[16,2048]{1,0:T(8,128)S(1)}, u32[]{:S(2)}, u32[]{:S(2)}) %collective-permute-start.9) | collective-permute-done | bytes 131104 | tf_op jit(solution)/shard_map/ppermute | solution.py:211
  83.8 4.2 %collective-permute-done.10 = f32[16,2048]{1,0:T(8,128)S(1)} collective-permute-done((f32[16,2048]{1,0:T(8,128)S(1)}, f32[16,2048]{1,0:T(8,128)S(1)}, u32[]{:S(2)}, u32[]{:S(2)}) %collective-permute-start.10) | collective-permute-done | bytes 131104 | tf_op jit(solution)/shard_map/ppermute | solution.py:211
  88.1 5.9 %factor.1.inverse_ref = f32[64,64]{1,0:T(8,128)S(1)} custom-call(f32[512,128]{1,0:T(8,128)S(1)} %pad_maximum_fusion.1.left_ref), custom_call_target="tpu_custom_call" | custom-call | tf_op jit(solution)/shard_map/factor/pallas_call | solution.py:146
  94.1 2.2 %copy-done.5 = bf16[1024,2048]{1,0:T(8,128)(2,1)S(1)} copy-done((bf16[1024,2048]{1,0:T(8,128)(2,1)S(1)}, bf16[1024,2048]{1,0:T(8,128)(2,1)}, u32[]{:S(2)}) %copy-start.5) | copy-done | bytes 4194328
  96.3 8.2 %finish.1 = (bf16[1024,2048]{1,0:T(8,128)(2,1)}, f32[64,2048]{1,0:T(8,128)}) custom-call(f32[512,128]{1,0:T(8,128)S(1)} %pad_maximum_fusion.1.left_ref, f32[64,64]{1,0:T(8,128)S(1)} %factor.1.inverse_ref, f32[64,2048]{1,0:T(8,128)S(1)} %pad_maximum_fusion.sum_ref, bf16[1024,2048]{1,0:T(8,128)(2,1)S(1)} %copy-done.2, bf16[1024,2048]{1,0:T(8,128)(2,1)S(1)} %copy-done.5), custom_call_target="tpu_custom_call" | custom-call | tf_op jit(solution)/shard_map/finish/pallas_call | solution.py:186
  (44 shorter events, 11.3 us)
Async XLA Ops:
  0.6 2.2 %copy-start.6 = (bf16[1024,2048]{1,0:T(8,128)(2,1)S(1)}, bf16[1024,2048]{1,0:T(8,128)(2,1)}, u32[]{:S(2)}) copy-start(bf16[1024,2048]{1,0:T(8,128)(2,1)} %hid_ref.1) | copy-start | bytes 12582916
  2.8 2.2 %copy-start.7 = (bf16[1024,2048]{1,0:T(8,128)(2,1)S(1)}, bf16[1024,2048]{1,0:T(8,128)(2,1)}, u32[]{:S(2)}) copy-start(bf16[1024,2048]{1,0:T(8,128)(2,1)} %err_ref.1) | copy-start | bytes 12582916
  5.0 1.6 %copy-start.8 = (bf16[1024,1024]{1,0:T(8,128)(2,1)S(1)}, bf16[1024,1024]{1,0:T(8,128)(2,1)}, u32[]{:S(2)}) copy-start(bf16[1024,1024]{1,0:T(8,128)(2,1)} %grad_ref.1) | copy-start | bytes 6291460
  6.6 1.0 copy-start.9
  27.0 2.0 %copy-start = (bf16[1024,2048]{1,0:T(8,128)(2,1)}, bf16[1024,2048]{1,0:T(8,128)(2,1)S(1)}, u32[]{:S(2)}) copy-start(bf16[1024,2048]{1,0:T(8,128)(2,1)S(1)} %get-tuple-element.8.high_ref) | copy-start | bytes 12582916
  29.0 1.9 %copy-start.3 = (bf16[1024,2048]{1,0:T(8,128)(2,1)}, bf16[1024,2048]{1,0:T(8,128)(2,1)S(1)}, u32[]{:S(2)}) copy-start(bf16[1024,2048]{1,0:T(8,128)(2,1)S(1)} %get-tuple-element.9.low_ref) | copy-start | bytes 12582916
  31.0 1.5 %collective-permute-start = (f32[256,128]{1,0:T(8,128)S(1)}, f32[256,128]{1,0:T(8,128)S(1)}, u32[]{:S(2)}, u32[]{:S(2)}) collective-permute-start(f32[256,128]{1,0:T(8,128)S(1)} %slice_select_fusion.2), channel_id=1, source_target_pairs={{0,4},{1,5},{2,6},{3,7},{4,0},{5,1},{6,2},{7,3},{8,12},{9,13},{10,... | collective-permute-start | bytes 393224 | tf_op jit(solution)/shard_map/ppermute | solution.py:211
  32.6 5.3 %collective-permute-start.1 = (f32[128,128]{1,0:T(8,128)S(1)}, f32[128,128]{1,0:T(8,128)S(1)}, u32[]{:S(2)}, u32[]{:S(2)}) collective-permute-start(f32[128,128]{1,0:T(8,128)S(1)} %slice_select_fusion.3), channel_id=1, source_target_pairs={{0,1},{1,0},{2,3},{3,2},{4,5},{5,4},{6,7},{7,6},{8,9},{9,8},{10,11... | collective-permute-start | bytes 196616 | tf_op jit(solution)/shard_map/ppermute | solution.py:211
  37.9 4.3 %collective-permute-start.2 = (f32[128,128]{1,0:T(8,128)S(1)}, f32[128,128]{1,0:T(8,128)S(1)}, u32[]{:S(2)}, u32[]{:S(2)}) collective-permute-start(f32[128,128]{1,0:T(8,128)S(1)} %select_add_fusion.3), channel_id=1, source_target_pairs={{0,2},{1,3},{2,0},{3,1},{4,6},{5,7},{6,4},{7,5},{8,10},{9,11},{10,... | collective-permute-start | bytes 196616 | tf_op jit(solution)/shard_map/ppermute | solution.py:211
  42.3 4.3 %collective-permute-start.3 = (f32[128,128]{1,0:T(8,128)S(1)}, f32[128,128]{1,0:T(8,128)S(1)}, u32[]{:S(2)}, u32[]{:S(2)}) collective-permute-start(f32[128,128]{1,0:T(8,128)S(1)} %add.31), channel_id=1, source_target_pairs={{0,8},{1,9},{2,10},{3,11},{4,12},{5,13},{6,14},{7,15},{8,0},{9,1},... | collective-permute-start | bytes 196616 | tf_op jit(solution)/shard_map/ppermute | solution.py:211
  46.6 5.9 %collective-permute-start.4 = (f32[128,128]{1,0:T(8,128)S(1)}, f32[128,128]{1,0:T(8,128)S(1)}, u32[]{:S(2)}, u32[]{:S(2)}) collective-permute-start(f32[128,128]{1,0:T(8,128)S(1)} %add.32), channel_id=1, source_target_pairs={{0,16},{1,17},{2,18},{3,19},{4,20},{5,21},{6,22},{7,23},{8,24},{9,... | collective-permute-start | bytes 196616 | tf_op jit(solution)/shard_map/ppermute | solution.py:211
  52.6 4.3 %collective-permute-start.5 = (f32[128,128]{1,0:T(8,128)S(1)}, f32[128,128]{1,0:T(8,128)S(1)}, u32[]{:S(2)}, u32[]{:S(2)}) collective-permute-start(f32[128,128]{1,0:T(8,128)S(1)} %add.33), channel_id=1, source_target_pairs={{0,1},{1,0},{2,3},{3,2},{4,5},{5,4},{6,7},{7,6},{8,9},{9,8},{10,11... | collective-permute-start | bytes 196616 | tf_op jit(solution)/shard_map/ppermute | solution.py:211
  56.9 1.4 %collective-permute-start.6 = (f32[256,128]{1,0:T(8,128)S(1)}, f32[256,128]{1,0:T(8,128)S(1)}, u32[]{:S(2)}, u32[]{:S(2)}) collective-permute-start(f32[256,128]{1,0:T(8,128)S(1)} %pad_maximum_fusion.3), channel_id=1, source_target_pairs={{0,4},{1,5},{2,6},{3,7},{4,0},{5,1},{6,2},{7,3},{8,12},{9,13},{10,... | collective-permute-start | bytes 393224 | tf_op jit(solution)/shard_map/ppermute | solution.py:211
  58.4 2.2 %copy-start.1 = (bf16[1024,2048]{1,0:T(8,128)(2,1)S(1)}, bf16[1024,2048]{1,0:T(8,128)(2,1)}, u32[]{:S(2)}) copy-start(bf16[1024,2048]{1,0:T(8,128)(2,1)} %copy-done) | copy-start | bytes 12582916
  60.6 2.2 %copy-start.4 = (bf16[1024,2048]{1,0:T(8,128)(2,1)S(1)}, bf16[1024,2048]{1,0:T(8,128)(2,1)}, u32[]{:S(2)}) copy-start(bf16[1024,2048]{1,0:T(8,128)(2,1)} %copy-done.3) | copy-start | bytes 12582916
  66.8 1.6 %collective-permute-start.7 = (f32[32,2048]{1,0:T(8,128)S(1)}, f32[32,2048]{1,0:T(8,128)S(1)}, u32[]{:S(2)}, u32[]{:S(2)}) collective-permute-start(f32[32,2048]{1,0:T(8,128)S(1)} %slice_select_fusion), channel_id=1, source_target_pairs={{0,4},{1,5},{2,6},{3,7},{4,0},{5,1},{6,2},{7,3},{8,12},{9,13},{10,... | collective-permute-start | bytes 786440 | tf_op jit(solution)/shard_map/ppermute | solution.py:211
  67.0 27.1 %copy-start.2 = (bf16[1024,2048]{1,0:T(8,128)(2,1)S(1)}, bf16[1024,2048]{1,0:T(8,128)(2,1)}, u32[]{:S(2)}) copy-start(bf16[1024,2048]{1,0:T(8,128)(2,1)} %copy-done) | copy-start | bytes 12582916
  68.5 5.6 %collective-permute-start.8 = (f32[16,2048]{1,0:T(8,128)S(1)}, f32[16,2048]{1,0:T(8,128)S(1)}, u32[]{:S(2)}, u32[]{:S(2)}) collective-permute-start(f32[16,2048]{1,0:T(8,128)S(1)} %slice_select_fusion.1), channel_id=1, source_target_pairs={{0,8},{1,9},{2,10},{3,11},{4,12},{5,13},{6,14},{7,15},{8,0},{9,1},... | collective-permute-start | bytes 393224 | tf_op jit(solution)/shard_map/ppermute | solution.py:211
  74.1 8.8 %collective-permute-start.9 = (f32[16,2048]{1,0:T(8,128)S(1)}, f32[16,2048]{1,0:T(8,128)S(1)}, u32[]{:S(2)}, u32[]{:S(2)}) collective-permute-start(f32[16,2048]{1,0:T(8,128)S(1)} %select_add_fusion.1), channel_id=1, source_target_pairs={{0,16},{1,17},{2,18},{3,19},{4,20},{5,21},{6,22},{7,23},{8,24},{9,... | collective-permute-start | bytes 393224 | tf_op jit(solution)/shard_map/ppermute | solution.py:211
  83.0 5.0 %collective-permute-start.10 = (f32[16,2048]{1,0:T(8,128)S(1)}, f32[16,2048]{1,0:T(8,128)S(1)}, u32[]{:S(2)}, u32[]{:S(2)}) collective-permute-start(f32[16,2048]{1,0:T(8,128)S(1)} %add.36), channel_id=1, source_target_pairs={{0,8},{1,9},{2,10},{3,11},{4,12},{5,13},{6,14},{7,15},{8,0},{9,1},... | collective-permute-start | bytes 393224 | tf_op jit(solution)/shard_map/ppermute | solution.py:211
  88.1 6.0 %collective-permute-start.11 = (f32[32,2048]{1,0:T(8,128)S(1)}, f32[32,2048]{1,0:T(8,128)S(1)}, u32[]{:S(2)}, u32[]{:S(2)}) collective-permute-start(f32[32,2048]{1,0:T(8,128)S(1)} %pad_maximum_fusion.2), channel_id=1, source_target_pairs={{0,4},{1,5},{2,6},{3,7},{4,0},{5,1},{6,2},{7,3},{8,12},{9,13},{10,... | collective-permute-start | bytes 786440 | tf_op jit(solution)/shard_map/ppermute | solution.py:211
  94.1 2.2 %copy-start.5 = (bf16[1024,2048]{1,0:T(8,128)(2,1)S(1)}, bf16[1024,2048]{1,0:T(8,128)(2,1)}, u32[]{:S(2)}) copy-start(bf16[1024,2048]{1,0:T(8,128)(2,1)} %copy-done.3) | copy-start | bytes 12582916
